TPU v7x, 32 devices: a whole 2x2x4 slice. The times are simulated.
32 devices in a mesh: parts: 2 (over y), blk: 4 (over z), sub: 4 (over x, core).
Axes of the slice: x: 2, y: 2, z: 4, core: 2. Of those that a mesh axis runs over, the one named last changes fastest.
Arguments:
- readings: float32 [2, 24576, 256], P(None, ('parts', 'blk', 'sub')), parts along dimension 1, may hold values from -6 to 6
- coverage: int32 [2, 24576, 256], P(None, ('parts', 'blk', 'sub')), parts along dimension 1, may hold values 0 or 1
- pixel_factors: float32 [24576, 256], P(('parts', 'blk', 'sub')), parts along dimension 0, may hold values from -1.5 to 1.5
- date_factors: float32 [2048, 256], P(('parts', 'blk', 'sub')), parts along dimension 0, may hold values from -1.5 to 1.5
Outputs:
- pixel_out: float32 [24576, 256], P(('parts', 'blk', 'sub')), parts along dimension 0
- date_out: float32 [2048, 256], P(('parts', 'blk', 'sub')), parts along dimension 0
There are 2 independent parts, one for each index of `parts`. A program takes and returns all parts, laid end to end along the dimension named above; each array names one. Nothing has to cross between parts.
All inputs are finite; a program needn't handle non-finite values. No bound on the sum of `coverage` on one device may be relied on, other than what follows from the above.
Results may differ from a plain program's by a relative error of at most 0.0001.
Values sent between devices are 32-bit elements; how exact they have to be, the bound alone decides.
No kernel may reach another device: no remote copies, remote signals or barrier semaphores. Data moves between devices by JAX's collectives and lax.ppermute only.
A program may use at most 64 MiB of HBM per device.

v0:
```python
import jax
import jax.numpy as jnp
from jax import lax
from jax.sharding import PartitionSpec as P

STRATA = 2
step_size = 0.05
ridge = 0.1
epsilon = 1e-06


def from_behind(value, axis, steps):
    count = lax.axis_size(axis)
    pairs = [(source, (source + steps) % count) for source in range(count)]
    return lax.ppermute(value, axis, pairs)


def local_terms(values, weights, strip, block):
    hp = lax.Precision.HIGHEST
    predicted = lax.dot_general(strip, block, (((1,), (1,)), ((), ())), precision=hp)
    errors = weights * (values - predicted)
    pixel_grad = -jnp.dot(errors, block, precision=hp) + ridge * strip
    date_part = -lax.dot_general(errors, strip, (((0,), (0,)), ((), ())), precision=hp)
    return (pixel_grad, date_part)


def on_device(readings, coverage, pixel_factors, date_factors):
    strip = pixel_factors
    share_rows = date_factors.shape[0]
    groups = lax.axis_size("sub")
    block_rows = share_rows * groups
    pixel_count = strip.shape[0] * groups * strip.shape[1]
    date_count = block_rows * strip.shape[1]
    share = date_factors
    for stratum in range(STRATA):
        block = lax.all_gather(share, "sub", axis=0, tiled=True)
        values = readings[stratum]
        weights = coverage[stratum].astype(jnp.float32)
        pixel_grad, date_part = local_terms(values, weights, strip, block)
        own_part = lax.psum_scatter(date_part, "sub", scatter_dimension=0, tiled=True)
        date_grad = own_part + ridge * share
        pixel_sq, date_sq = lax.psum(
            (jnp.sum(pixel_grad * pixel_grad), jnp.sum(date_grad * date_grad)), "sub"
        )
        strip = strip - step_size * pixel_grad / jnp.sqrt(pixel_sq / pixel_count + epsilon)
        share = share - step_size * date_grad / jnp.sqrt(date_sq / date_count + epsilon)
        share = from_behind(share, "blk", 1)
    return (strip, share)


def solution(mesh):
    in_specs = (
        P(None, ("parts", "blk", "sub"), None),
        P(None, ("parts", "blk", "sub"), None),
        P(("parts", "blk", "sub"), None),
        P(("parts", "blk", "sub"), None),
    )
    out_specs = (P(("parts", "blk", "sub"), None), P(("parts", "blk", "sub"), None))
    return jax.shard_map(
        on_device, mesh=mesh, in_specs=in_specs, out_specs=out_specs, check_vma=False
    )
```

profile of v0, /device:TPU:0, one launch (start us, length us, event | category | flops | bytes accessed | tf_op | source)
XLA Modules:
  0.0 109.8 jit_solution(7786691914013596123)
XLA Ops:
  7.2 0.0 reduce-scatter.3.cloned.1.call-start
  7.2 7.4 %all_gather.6 = f32[256,256]{1,0:T(8,128)S(1)} all-gather(f32[64,256]{1,0:T(8,128)} %param.7), channel_id=1, replica_groups=mesh['parts'=2,'blk'=4,'sub'=4] {'sub'}, dimensions={0}, use_global_device_ids=true | all-gather | bytes 327680 | tf_op jit(solution)/shard_map/all_gather | solution.py:36
  14.6 0.0 copy-start
  14.6 2.5 %fusion.3 = f32[768,256]{1,0:T(8,128)S(1)} fusion(f32[768,256]{1,0:T(8,128)} %param.6, f32[256,256]{1,0:T(8,128)S(1)} %all_gather.6, f32[2,768,256]{2,1,0:T(8,128)} %param.4, s32[2,768,256]{2,1,0:T(8,128)} %param.5), kind=kOutput, calls=%fused_computation.7 | convolution fusion | flops 604569600 | bytes 3407872 | tf_op jit(solution)/shard_map/dot_general | solution.py:20
  17.1 0.0 copy-done
  17.2 2.1 %convolution_negate_fusion.3 = f32[256,256]{1,0:T(8,128)} fusion(f32[768,256]{1,0:T(8,128)S(1)} %fusion.3, f32[768,256]{1,0:T(8,128)S(1)} %copy-done), kind=kOutput, calls=%fused_computation.9 | convolution fusion | flops 604045312 | bytes 1835008 | tf_op jit(solution)/shard_map/dot_general | solution.py:23
  19.3 0.0 copy-start.1
  19.3 0.0 reduce-scatter.3.cloned.1.call-update
  19.3 0.0 reduce-scatter.5.cloned.1.call-start
  19.4 1.4 %multiply_reduce_fusion.1 = (f32[]{:T(128)}, f32[768,256]{1,0:T(8,128)S(1)}) fusion(f32[768,256]{1,0:T(8,128)S(1)} %copy-done, f32[768,256]{1,0:T(8,128)S(1)} %fusion.3, f32[256,256]{1,0:T(8,128)S(1)} %all_gather.6), kind=kOutput, calls=%fused_computation.13 | convolution fusion | flops 604962816 | bytes 2621444 | tf_op jit(solution)/shard_map/dot_general | solution.py:22
  20.8 20.0 %reduce-scatter.3.cloned.1.call-done = f32[64,256]{1,0:T(8,128)} async-done(((f32[256,256]{1,0:T(8,128)}), f32[64,256]{1,0:T(8,128)}) %reduce-scatter.3.cloned.1.call-update) | async-done | bytes 65552 | tf_op jit(solution)/shard_map/reduce_scatter | solution.py:40
  40.8 0.0 copy-done.1
  40.8 1.5 %multiply_reduce_fusion.3 = f32[]{:T(128)} fusion(f32[64,256]{1,0:T(8,128)} %reduce-scatter.3.cloned.1.call-done, f32[64,256]{1,0:T(8,128)S(1)} %copy-done.1), kind=kLoop, calls=%fused_computation.18 | loop fusion | flops 65535 | bytes 131076 | tf_op jit(solution)/shard_map/reduce_sum | solution.py:43
  42.3 6.4 %all-reduce.1 = (f32[]{:T(128)}, f32[]{:T(128)}) all-reduce(f32[]{:T(128)} %get-tuple-element.6, f32[]{:T(128)} %multiply_reduce_fusion.3), channel_id=1, replica_groups=mesh['parts'=2,'blk'=4,'sub'=4] {'sub'}, use_global_device_ids=true, to_apply=%region_1.0 | all-reduce | flops 2 | bytes 16 | tf_op jit(solution)/shard_map/psum | solution.py:42
  50.0 0.9 divide_subtract_fusion.3
  50.9 1.7 %collective-permute-start = (f32[64,256]{1,0:T(8,128)S(1)}, f32[64,256]{1,0:T(8,128)S(1)}, u32[]{:S(2)}, u32[]{:S(2)}) collective-permute-start(f32[64,256]{1,0:T(8,128)S(1)} %divide_subtract_fusion.3), channel_id=1, source_target_pairs={{0,4},{4,8},{8,12},{12,0},{1,5},{5,9},{9,13},{13,1},{2,6},{6,10},{... | collective-permute-start | bytes 196616 | tf_op jit(solution)/shard_map/ppermute | solution.py:15
  52.6 0.1 divide_subtract_fusion.1
  52.7 4.3 %collective-permute-done = f32[64,256]{1,0:T(8,128)S(1)} collective-permute-done((f32[64,256]{1,0:T(8,128)S(1)}, f32[64,256]{1,0:T(8,128)S(1)}, u32[]{:S(2)}, u32[]{:S(2)}) %collective-permute-start) | collective-permute-done | bytes 65568 | tf_op jit(solution)/shard_map/ppermute | solution.py:15
  57.0 5.8 %all_gather.7 = f32[256,256]{1,0:T(8,128)S(1)} all-gather(f32[64,256]{1,0:T(8,128)S(1)} %collective-permute-done), channel_id=1, replica_groups=mesh['parts'=2,'blk'=4,'sub'=4] {'sub'}, dimensions={0}, use_global_device_ids=true | all-gather | bytes 327680 | tf_op jit(solution)/shard_map/all_gather | solution.py:36
  62.8 2.2 %fusion.2 = f32[768,256]{1,0:T(8,128)S(1)} fusion(f32[768,256]{1,0:T(8,128)S(1)} %divide_subtract_fusion.1, f32[256,256]{1,0:T(8,128)S(1)} %all_gather.7, f32[2,768,256]{2,1,0:T(8,128)} %param.4, s32[2,768,256]{2,1,0:T(8,128)} %param.5), kind=kOutput, calls=%fused_computation.5 | convolution fusion | flops 604569600 | bytes 3407872 | tf_op jit(solution)/shard_map/dot_general | solution.py:20
  65.0 2.1 %convolution_negate_fusion.2 = f32[256,256]{1,0:T(8,128)} fusion(f32[768,256]{1,0:T(8,128)S(1)} %fusion.2, f32[768,256]{1,0:T(8,128)S(1)} %divide_subtract_fusion.1), kind=kOutput, calls=%fused_computation.8 | convolution fusion | flops 604045312 | bytes 1835008 | tf_op jit(solution)/shard_map/dot_general | solution.py:23
  67.1 0.0 reduce-scatter.5.cloned.1.call-update
  67.1 1.4 %multiply_reduce_fusion = (f32[]{:T(128)}, f32[768,256]{1,0:T(8,128)S(1)}) fusion(f32[768,256]{1,0:T(8,128)S(1)} %divide_subtract_fusion.1, f32[768,256]{1,0:T(8,128)S(1)} %fusion.2, f32[256,256]{1,0:T(8,128)S(1)} %all_gather.7), kind=kOutput, calls=%fused_computation.11 | convolution fusion | flops 604962816 | bytes 2621444 | tf_op jit(solution)/shard_map/dot_general | solution.py:22
  68.5 17.6 %reduce-scatter.5.cloned.1.call-done = f32[64,256]{1,0:T(8,128)} async-done(((f32[256,256]{1,0:T(8,128)}), f32[64,256]{1,0:T(8,128)}) %reduce-scatter.5.cloned.1.call-update) | async-done | bytes 65552 | tf_op jit(solution)/shard_map/reduce_scatter | solution.py:40
  86.1 1.5 %multiply_reduce_fusion.2 = f32[]{:T(128)} fusion(f32[64,256]{1,0:T(8,128)} %reduce-scatter.5.cloned.1.call-done, f32[64,256]{1,0:T(8,128)S(1)} %collective-permute-done), kind=kLoop, calls=%fused_computation.15 | loop fusion | flops 65535 | bytes 131076 | tf_op jit(solution)/shard_map/reduce_sum | solution.py:43
  87.6 6.4 %all-reduce = (f32[]{:T(128)}, f32[]{:T(128)}) all-reduce(f32[]{:T(128)} %get-tuple-element.8, f32[]{:T(128)} %multiply_reduce_fusion.2), channel_id=1, replica_groups=mesh['parts'=2,'blk'=4,'sub'=4] {'sub'}, use_global_device_ids=true, to_apply=%region_6.0 | all-reduce | flops 2 | bytes 16 | tf_op jit(solution)/shard_map/psum | solution.py:42
  95.3 0.9 divide_subtract_fusion.2
  96.2 1.7 %collective-permute-start.1 = (f32[64,256]{1,0:T(8,128)S(1)}, f32[64,256]{1,0:T(8,128)S(1)}, u32[]{:S(2)}, u32[]{:S(2)}) collective-permute-start(f32[64,256]{1,0:T(8,128)S(1)} %divide_subtract_fusion.2), channel_id=1, source_target_pairs={{0,4},{4,8},{8,12},{12,0},{1,5},{5,9},{9,13},{13,1},{2,6},{6,10},{... | collective-permute-start | bytes 196616 | tf_op jit(solution)/shard_map/ppermute | solution.py:15
  97.9 1.0 divide_subtract_fusion
  98.9 3.4 %collective-permute-done.1 = f32[64,256]{1,0:T(8,128)S(1)} collective-permute-done((f32[64,256]{1,0:T(8,128)S(1)}, f32[64,256]{1,0:T(8,128)S(1)}, u32[]{:S(2)}, u32[]{:S(2)}) %collective-permute-start.1) | collective-permute-done | bytes 65568 | tf_op jit(solution)/shard_map/ppermute | solution.py:15
  102.3 0.6 copy.7
Async XLA Ops:
  7.2 33.6 %reduce-scatter.3.cloned.1.call-start = ((), (), s32[]{:S(2)}) async-start(), calls=%async_computation.2 | async-start | bytes 327680 | tf_op jit(solution)/shard_map/reduce_scatter | solution.py:40
  14.6 2.5 %copy-start = (f32[768,256]{1,0:T(8,128)S(1)}, f32[768,256]{1,0:T(8,128)}, u32[]{:S(2)}) copy-start(f32[768,256]{1,0:T(8,128)} %param.6) | copy-start | bytes 2359300
  19.3 21.5 %copy-start.1 = (f32[64,256]{1,0:T(8,128)S(1)}, f32[64,256]{1,0:T(8,128)}, u32[]{:S(2)}) copy-start(f32[64,256]{1,0:T(8,128)} %param.7) | copy-start | bytes 196612
  19.3 66.8 %reduce-scatter.5.cloned.1.call-start = ((), (), s32[]{:S(2)}) async-start(), calls=%async_computation.3 | async-start | bytes 327680 | tf_op jit(solution)/shard_map/reduce_scatter | solution.py:40
  50.9 6.1 %collective-permute-start = (f32[64,256]{1,0:T(8,128)S(1)}, f32[64,256]{1,0:T(8,128)S(1)}, u32[]{:S(2)}, u32[]{:S(2)}) collective-permute-start(f32[64,256]{1,0:T(8,128)S(1)} %divide_subtract_fusion.3), channel_id=1, source_target_pairs={{0,4},{4,8},{8,12},{12,0},{1,5},{5,9},{9,13},{13,1},{2,6},{6,10},{... | collective-permute-start | bytes 196616 | tf_op jit(solution)/shard_map/ppermute | solution.py:15
  96.2 6.1 %collective-permute-start.1 = (f32[64,256]{1,0:T(8,128)S(1)}, f32[64,256]{1,0:T(8,128)S(1)}, u32[]{:S(2)}, u32[]{:S(2)}) collective-permute-start(f32[64,256]{1,0:T(8,128)S(1)} %divide_subtract_fusion.2), channel_id=1, source_target_pairs={{0,4},{4,8},{8,12},{12,0},{1,5},{5,9},{9,13},{13,1},{2,6},{6,10},{... | collective-permute-start | bytes 196616 | tf_op jit(solution)/shard_map/ppermute | solution.py:15
Sparse Core Ops, SparseCore 0:
  19.4 21.3 reduce-scatter.2
  67.2 18.8 reduce-scatter.4
where the time goes:
time: 110 us
  waiting for transfers between devices  45.3 us (41%)
  blocking collectives  25.9 us (24%)
  between operations  16.8 us (15%)
  matrix products  11.7 us (11%)
  other arithmetic  5.73 us (5%)
  starting transfers between devices  3.54 us (3%)
    reduce_scatter x2, waiting for transfers between devices, on_device(): lax.psum_scatter(date_part, 'sub', scatter_dimension=0, tiled=True)  37.6 us
    all_gather x2, blocking collectives, on_device(): block = lax.all_gather(share, 'sub', axis=0, tiled=True)  13.2 us
    psum x2, blocking collectives, on_device(): lax.psum((jnp.sum(pixel_grad * pixel_grad), jnp.sum(date_grad * date_grad...  12.7 us
    ppermute x2, waiting for transfers between devices, from_behind(): return lax.ppermute(value, axis, pairs)  7.68 us
    dot_general x2, matrix products, local_terms(): lax.dot_general(strip, block, (((1,), (1,)), ((), ())), precision=hp)  4.68 us
    dot_general x2, matrix products, local_terms(): lax.dot_general(errors, strip, (((0,), (0,)), ((), ())), precision=hp)  4.24 us
    ppermute x2, starting transfers between devices, from_behind(): return lax.ppermute(value, axis, pairs)  3.46 us
    reduce_sum x2, other arithmetic, on_device(): jnp.sum(date_grad * date_grad)  2.92 us
  transfers between devices with their start and end apart: 4, of which 4 were waited for; matrix products, arithmetic and copies ran while one was open for 4% of the time, Pallas kernels for 0%

commit v1 on v0

--- a/solution.py
+++ b/solution.py
@@ -33,7 +33,14 @@
     date_count = block_rows * strip.shape[1]
     share = date_factors
     for stratum in range(STRATA):
-        block = lax.all_gather(share, "sub", axis=0, tiled=True)
+        ring = [share]
+        for hop in range(3):
+            ring.append(lax.ppermute(ring[-1], "sub", [(dev, (dev + 1) % 4) for dev in range(4)]))
+        block = jnp.roll(
+            jnp.concatenate(ring[::-1], axis=0),
+            (lax.axis_index("sub") + 1) * ring[0].shape[0],
+            axis=0,
+        )
         values = readings[stratum]
         weights = coverage[stratum].astype(jnp.float32)
         pixel_grad, date_part = local_terms(values, weights, strip, block)

time: 110 us -> 120 us (1.091)
  waiting for transfers between devices: 45.3 us -> 65.8 us
  blocking collectives: 25.9 us -> 12.7 us
  other arithmetic: 5.73 us -> 7.34 us
  matrix products: 11.7 us -> 10.1 us
  local copies, waits for them, and re-layouts: 0.64 us -> 2.03 us
    ppermute x0 -> x6, waiting for transfers between devices: none -> 20.2 us  [on_device(): lax.ppermute(ring[-1], 'sub', [(dev, (dev + 1) % 4) for dev in range(4)])]
    all_gather x2 -> x0, blocking collectives: 13.2 us -> none  [on_device(): block = lax.all_gather(share, 'sub', axis=0, tiled=True)]
    dot_general x2, matrix products: 4.68 us -> 3.04 us  [local_terms(): lax.dot_general(strip, block, (((1,), (1,)), ((), ())), precision=hp)]
    concatenate x0 -> x2, other arithmetic: none -> 1.62 us  [on_device(): jnp.roll(jnp.concatenate(ring[::-1], axis=0), (lax.axis_index('sub') + 1)...]
  transfers between devices with their start and end apart: 4 -> 10, of which waited for: 4 -> 10; matrix products, arithmetic and copies ran while one was open for 4% -> 4% of each run, Pallas kernels for 0% -> 0%
where the time goes in v1:
time: 120 us; the launch traced here: 119 us
  waiting for transfers between devices  65.8 us (55%)
  between operations  16.9 us (14%)
  blocking collectives  12.7 us (11%)
  matrix products  10.1 us (8%)
  other arithmetic  7.34 us (6%)
  starting transfers between devices  4.33 us (4%)
  local copies, waits for them, and re-layouts  2.03 us (2%)
    reduce_scatter x2, waiting for transfers between devices, on_device(): lax.psum_scatter(date_part, 'sub', scatter_dimension=0, tiled=True)  37.8 us
    ppermute x6, waiting for transfers between devices, on_device(): lax.ppermute(ring[-1], 'sub', [(dev, (dev + 1) % 4) for dev in range(4)])  20.2 us
    psum x2, blocking collectives, on_device(): lax.psum((jnp.sum(pixel_grad * pixel_grad), jnp.sum(date_grad * date_grad...  12.7 us
    ppermute x2, waiting for transfers between devices, from_behind(): return lax.ppermute(value, axis, pairs)  7.76 us
    dot_general x2, matrix products, local_terms(): lax.dot_general(errors, strip, (((0,), (0,)), ((), ())), precision=hp)  3.63 us
    ppermute x2, starting transfers between devices, from_behind(): return lax.ppermute(value, axis, pairs)  3.48 us
    dot_general x2, matrix products, local_terms(): pixel_grad = -jnp.dot(errors, block, precision=hp) + ridge * strip  3.44 us
    dot_general x2, matrix products, local_terms(): lax.dot_general(strip, block, (((1,), (1,)), ((), ())), precision=hp)  3.04 us
  transfers between devices with their start and end apart: 10, of which 10 were waited for; matrix products, arithmetic and copies ran while one was open for 4% of the time, Pallas kernels for 0%

profile of v1, /device:TPU:0, one launch (start us, length us, event | category | flops | bytes accessed | tf_op | source)
XLA Modules:
  0.0 119.2 jit_solution(16735285917343817295)
XLA Ops:
  7.2 0.5 collective-permute-start
  7.8 4.1 %collective-permute-done = f32[64,256]{1,0:T(8,128)S(1)} collective-permute-done((f32[64,256]{1,0:T(8,128)}, f32[64,256]{1,0:T(8,128)S(1)}, u32[]{:S(2)}, u32[]{:S(2)}) %collective-permute-start) | collective-permute-done | bytes 65568 | tf_op jit(solution)/shard_map/ppermute | solution.py:38
  12.0 3.5 %collective-permute-done.1 = f32[64,256]{1,0:T(8,128)S(1)} collective-permute-done((f32[64,256]{1,0:T(8,128)S(1)}, f32[64,256]{1,0:T(8,128)S(1)}, u32[]{:S(2)}, u32[]{:S(2)}) %collective-permute-start.1) | collective-permute-done | bytes 65568 | tf_op jit(solution)/shard_map/ppermute | solution.py:38
  15.6 0.3 copy.9
  15.9 0.3 copy-done.2
  16.2 0.6 slice-done.1
  17.0 2.3 %collective-permute-done.2 = f32[64,256]{1,0:T(8,128)} collective-permute-done((f32[64,256]{1,0:T(8,128)S(1)}, f32[64,256]{1,0:T(8,128)}, u32[]{:S(2)}, u32[]{:S(2)}) %collective-permute-start.2) | collective-permute-done | bytes 65568 | tf_op jit(solution)/shard_map/ppermute | solution.py:38
  19.3 1.2 %fusion.15 = f32[256,256]{1,0:T(8,128)S(1)} fusion(s32[]{:T(128)S(6)} %select_n.13, f32[64,256]{1,0:T(8,128)} %collective-permute-done.2, f32[64,256]{1,0:T(8,128)} %copy-done.2, f32[64,256]{1,0:T(8,128)S(1)} %collective-permute-done, f32[64,256]{1,0:T(8,128)S(1)} %copy-done.1), kind=kLoop, calls=%fused_computation.41 | loop fusion | flops 458752 | bytes 524292 | tf_op jit(solution)/shard_map/jit(_roll_dynamic)/concatenate | solution.py:39
  20.5 0.8 fusion.1
  21.4 1.5 %convolution_negate_fusion.3 = f32[256,256]{1,0:T(8,128)} fusion(f32[768,256]{0,1:T(8,128)S(1)} %fusion.1, f32[768,256]{1,0:T(8,128)S(1)} %copy-done), kind=kOutput, calls=%fused_computation.10 | convolution fusion | flops 604045312 | bytes 1835008 | tf_op jit(solution)/shard_map/dot_general | solution.py:23
  23.0 2.0 %multiply_reduce_fusion.1 = (f32[]{:T(128)}, f32[768,256]{1,0:T(8,128)S(1)}) fusion(f32[768,256]{1,0:T(8,128)S(1)} %copy-done, f32[768,256]{0,1:T(8,128)S(1)} %fusion.1, f32[256,256]{1,0:T(8,128)S(1)} %fusion.15), kind=kOutput, calls=%fused_computation.14 | convolution fusion | flops 604962816 | bytes 2621444 | tf_op jit(solution)/shard_map/dot_general | solution.py:22
  25.0 20.2 %reduce-scatter.3.cloned.1.call-done = f32[64,256]{1,0:T(8,128)} async-done(((f32[256,256]{1,0:T(8,128)}), f32[64,256]{1,0:T(8,128)}) %reduce-scatter.3.cloned.1.call-update) | async-done | bytes 65552 | tf_op jit(solution)/shard_map/reduce_scatter | solution.py:47
  45.2 1.5 %multiply_reduce_fusion.3 = f32[]{:T(128)} fusion(f32[64,256]{1,0:T(8,128)} %reduce-scatter.3.cloned.1.call-done, f32[64,256]{1,0:T(8,128)S(1)} %copy-done.1), kind=kLoop, calls=%fused_computation.49 | loop fusion | flops 65535 | bytes 131076 | tf_op jit(solution)/shard_map/reduce_sum | solution.py:50
  46.7 6.4 %all-reduce.1 = (f32[]{:T(128)}, f32[]{:T(128)}) all-reduce(f32[]{:T(128)} %get-tuple-element.7, f32[]{:T(128)} %multiply_reduce_fusion.3), channel_id=1, replica_groups=mesh['parts'=2,'blk'=4,'sub'=4] {'sub'}, use_global_device_ids=true, to_apply=%region_1.3 | all-reduce | flops 2 | bytes 16 | tf_op jit(solution)/shard_map/psum | solution.py:49
  53.7 0.9 divide_subtract_fusion.3
  54.6 1.8 %collective-permute-start.3 = (f32[64,256]{1,0:T(8,128)S(1)}, f32[64,256]{1,0:T(8,128)S(1)}, u32[]{:S(2)}, u32[]{:S(2)}) collective-permute-start(f32[64,256]{1,0:T(8,128)S(1)} %divide_subtract_fusion.3), channel_id=1, source_target_pairs={{0,4},{4,8},{8,12},{12,0},{1,5},{5,9},{9,13},{13,1},{2,6},{6,10},{... | collective-permute-start | bytes 196616 | tf_op jit(solution)/shard_map/ppermute | solution.py:15
  56.3 4.4 %collective-permute-done.3 = f32[64,256]{1,0:T(8,128)S(1)} collective-permute-done((f32[64,256]{1,0:T(8,128)S(1)}, f32[64,256]{1,0:T(8,128)S(1)}, u32[]{:S(2)}, u32[]{:S(2)}) %collective-permute-start.3) | collective-permute-done | bytes 65568 | tf_op jit(solution)/shard_map/ppermute | solution.py:15
  60.7 3.7 %collective-permute-done.4 = f32[64,256]{1,0:T(8,128)S(1)} collective-permute-done((f32[64,256]{1,0:T(8,128)S(1)}, f32[64,256]{1,0:T(8,128)S(1)}, u32[]{:S(2)}, u32[]{:S(2)}) %collective-permute-start.4) | collective-permute-done | bytes 65568 | tf_op jit(solution)/shard_map/ppermute | solution.py:38
  65.1 3.0 %collective-permute-done.5 = f32[64,256]{1,0:T(8,128)S(1)} collective-permute-done((f32[64,256]{1,0:T(8,128)S(1)}, f32[64,256]{1,0:T(8,128)S(1)}, u32[]{:S(2)}, u32[]{:S(2)}) %collective-permute-start.5) | collective-permute-done | bytes 65568 | tf_op jit(solution)/shard_map/ppermute | solution.py:38
  68.2 3.6 %collective-permute-done.6 = f32[64,256]{1,0:T(8,128)S(1)} collective-permute-done((f32[64,256]{1,0:T(8,128)S(1)}, f32[64,256]{1,0:T(8,128)S(1)}, u32[]{:S(2)}, u32[]{:S(2)}) %collective-permute-start.6) | collective-permute-done | bytes 65568 | tf_op jit(solution)/shard_map/ppermute | solution.py:38
  71.8 0.4 fusion.8
  72.2 2.2 %fusion.4 = f32[768,256]{1,0:T(8,128)S(1)} fusion(f32[768,256]{1,0:T(8,128)S(1)} %divide_subtract_fusion.1, f32[256,256]{1,0:T(8,128)S(1)} %fusion.8, f32[2,768,256]{2,1,0:T(8,128)} %param.6, s32[2,768,256]{2,1,0:T(8,128)} %param.7), kind=kOutput, calls=%fused_computation.8 | convolution fusion | flops 604569600 | bytes 3407872 | tf_op jit(solution)/shard_map/dot_general | solution.py:20
  74.4 2.1 %convolution_negate_fusion.2 = f32[256,256]{1,0:T(8,128)} fusion(f32[768,256]{1,0:T(8,128)S(1)} %fusion.4, f32[768,256]{1,0:T(8,128)S(1)} %divide_subtract_fusion.1), kind=kOutput, calls=%fused_computation.9 | convolution fusion | flops 604045312 | bytes 1835008 | tf_op jit(solution)/shard_map/dot_general | solution.py:23
  76.5 1.4 %multiply_reduce_fusion = (f32[]{:T(128)}, f32[768,256]{1,0:T(8,128)S(1)}) fusion(f32[768,256]{1,0:T(8,128)S(1)} %divide_subtract_fusion.1, f32[768,256]{1,0:T(8,128)S(1)} %fusion.4, f32[256,256]{1,0:T(8,128)S(1)} %fusion.8), kind=kOutput, calls=%fused_computation.12 | convolution fusion | flops 604962816 | bytes 2621444 | tf_op jit(solution)/shard_map/dot_general | solution.py:22
  78.0 17.6 %reduce-scatter.5.cloned.1.call-done = f32[64,256]{1,0:T(8,128)} async-done(((f32[256,256]{1,0:T(8,128)}), f32[64,256]{1,0:T(8,128)}) %reduce-scatter.5.cloned.1.call-update) | async-done | bytes 65552 | tf_op jit(solution)/shard_map/reduce_scatter | solution.py:47
  95.5 1.5 %multiply_reduce_fusion.2 = f32[]{:T(128)} fusion(f32[64,256]{1,0:T(8,128)} %reduce-scatter.5.cloned.1.call-done, f32[64,256]{1,0:T(8,128)S(1)} %collective-permute-done.3), kind=kLoop, calls=%fused_computation.46 | loop fusion | flops 65535 | bytes 131076 | tf_op jit(solution)/shard_map/reduce_sum | solution.py:50
  97.0 6.4 %all-reduce = (f32[]{:T(128)}, f32[]{:T(128)}) all-reduce(f32[]{:T(128)} %get-tuple-element.9, f32[]{:T(128)} %multiply_reduce_fusion.2), channel_id=1, replica_groups=mesh['parts'=2,'blk'=4,'sub'=4] {'sub'}, use_global_device_ids=true, to_apply=%region_6.8 | all-reduce | flops 2 | bytes 16 | tf_op jit(solution)/shard_map/psum | solution.py:49
  104.8 0.9 divide_subtract_fusion.2
  105.6 1.7 %collective-permute-start.7 = (f32[64,256]{1,0:T(8,128)S(1)}, f32[64,256]{1,0:T(8,128)S(1)}, u32[]{:S(2)}, u32[]{:S(2)}) collective-permute-start(f32[64,256]{1,0:T(8,128)S(1)} %divide_subtract_fusion.2), channel_id=1, source_target_pairs={{0,4},{4,8},{8,12},{12,0},{1,5},{5,9},{9,13},{13,1},{2,6},{6,10},{... | collective-permute-start | bytes 196616 | tf_op jit(solution)/shard_map/ppermute | solution.py:15
  107.3 1.0 divide_subtract_fusion
  108.3 3.4 %collective-permute-done.7 = f32[64,256]{1,0:T(8,128)S(1)} collective-permute-done((f32[64,256]{1,0:T(8,128)S(1)}, f32[64,256]{1,0:T(8,128)S(1)}, u32[]{:S(2)}, u32[]{:S(2)}) %collective-permute-start.7) | collective-permute-done | bytes 65568 | tf_op jit(solution)/shard_map/ppermute | solution.py:15
  111.7 0.6 copy.11
  (19 shorter events, 0.7 us)
Async XLA Ops:
  7.2 8.4 %slice-start = ((f32[2,768,256]{2,1,0:T(8,128)}), f32[1,768,256]{2,1,0:T(8,128)S(1)}, s32[]{:S(2)}) async-start(f32[2,768,256]{2,1,0:T(8,128)} %param.6), calls=%async_computation.4 | async-start | bytes 1572864 | tf_op jit(solution)/shard_map/slice | solution.py:44
  7.2 38.0 %reduce-scatter.3.cloned.1.call-start = ((), (), s32[]{:S(2)}) async-start(), calls=%async_computation.2 | async-start | bytes 327680 | tf_op jit(solution)/shard_map/reduce_scatter | solution.py:47
  7.2 4.6 %collective-permute-start = (f32[64,256]{1,0:T(8,128)}, f32[64,256]{1,0:T(8,128)S(1)}, u32[]{:S(2)}, u32[]{:S(2)}) collective-permute-start(f32[64,256]{1,0:T(8,128)} %param.9), channel_id=1, source_target_pairs={{0,1},{1,2},{2,3},{3,0},{4,5},{5,6},{6,7},{7,4},{8,9},{9,10},{10,1... | collective-permute-start | bytes 196616 | tf_op jit(solution)/shard_map/ppermute | solution.py:38
  11.8 3.7 %collective-permute-start.1 = (f32[64,256]{1,0:T(8,128)S(1)}, f32[64,256]{1,0:T(8,128)S(1)}, u32[]{:S(2)}, u32[]{:S(2)}) collective-permute-start(f32[64,256]{1,0:T(8,128)S(1)} %collective-permute-done), channel_id=1, source_target_pairs={{0,1},{1,2},{2,3},{3,0},{4,5},{5,6},{6,7},{7,4},{8,9},{9,10},{10,1... | collective-permute-start | bytes 196616 | tf_op jit(solution)/shard_map/ppermute | solution.py:38
  15.5 0.6 copy-start.2
  15.5 3.8 %collective-permute-start.2 = (f32[64,256]{1,0:T(8,128)S(1)}, f32[64,256]{1,0:T(8,128)}, u32[]{:S(2)}, u32[]{:S(2)}) collective-permute-start(f32[64,256]{1,0:T(8,128)S(1)} %collective-permute-done.1), channel_id=1, source_target_pairs={{0,1},{1,2},{2,3},{3,0},{4,5},{5,6},{6,7},{7,4},{8,9},{9,10},{10,1... | collective-permute-start | bytes 196616 | tf_op jit(solution)/shard_map/ppermute | solution.py:38
  15.6 1.1 slice-start.1
  16.2 3.2 %copy-start.1 = (f32[64,256]{1,0:T(8,128)S(1)}, f32[64,256]{1,0:T(8,128)}, u32[]{:S(2)}) copy-start(f32[64,256]{1,0:T(8,128)} %param.9) | copy-start | bytes 196612
  16.2 4.4 %copy-start = (f32[768,256]{1,0:T(8,128)S(1)}, f32[768,256]{1,0:T(8,128)}, u32[]{:S(2)}) copy-start(f32[768,256]{1,0:T(8,128)} %param.8) | copy-start | bytes 2359300
  22.9 72.6 %reduce-scatter.5.cloned.1.call-start = ((), (), s32[]{:S(2)}) async-start(), calls=%async_computation.3 | async-start | bytes 327680 | tf_op jit(solution)/shard_map/reduce_scatter | solution.py:47
  54.6 6.1 %collective-permute-start.3 = (f32[64,256]{1,0:T(8,128)S(1)}, f32[64,256]{1,0:T(8,128)S(1)}, u32[]{:S(2)}, u32[]{:S(2)}) collective-permute-start(f32[64,256]{1,0:T(8,128)S(1)} %divide_subtract_fusion.3), channel_id=1, source_target_pairs={{0,4},{4,8},{8,12},{12,0},{1,5},{5,9},{9,13},{13,1},{2,6},{6,10},{... | collective-permute-start | bytes 196616 | tf_op jit(solution)/shard_map/ppermute | solution.py:15
  60.7 3.7 %collective-permute-start.4 = (f32[64,256]{1,0:T(8,128)S(1)}, f32[64,256]{1,0:T(8,128)S(1)}, u32[]{:S(2)}, u32[]{:S(2)}) collective-permute-start(f32[64,256]{1,0:T(8,128)S(1)} %collective-permute-done.3), channel_id=1, source_target_pairs={{0,1},{1,2},{2,3},{3,0},{4,5},{5,6},{6,7},{7,4},{8,9},{9,10},{10,1... | collective-permute-start | bytes 196616 | tf_op jit(solution)/shard_map/ppermute | solution.py:38
  64.4 3.7 %collective-permute-start.5 = (f32[64,256]{1,0:T(8,128)S(1)}, f32[64,256]{1,0:T(8,128)S(1)}, u32[]{:S(2)}, u32[]{:S(2)}) collective-permute-start(f32[64,256]{1,0:T(8,128)S(1)} %collective-permute-done.4), channel_id=1, source_target_pairs={{0,1},{1,2},{2,3},{3,0},{4,5},{5,6},{6,7},{7,4},{8,9},{9,10},{10,1... | collective-permute-start | bytes 196616 | tf_op jit(solution)/shard_map/ppermute | solution.py:38
  68.1 3.7 %collective-permute-start.6 = (f32[64,256]{1,0:T(8,128)S(1)}, f32[64,256]{1,0:T(8,128)S(1)}, u32[]{:S(2)}, u32[]{:S(2)}) collective-permute-start(f32[64,256]{1,0:T(8,128)S(1)} %collective-permute-done.5), channel_id=1, source_target_pairs={{0,1},{1,2},{2,3},{3,0},{4,5},{5,6},{6,7},{7,4},{8,9},{9,10},{10,1... | collective-permute-start | bytes 196616 | tf_op jit(solution)/shard_map/ppermute | solution.py:38
  105.6 6.1 %collective-permute-start.7 = (f32[64,256]{1,0:T(8,128)S(1)}, f32[64,256]{1,0:T(8,128)S(1)}, u32[]{:S(2)}, u32[]{:S(2)}) collective-permute-start(f32[64,256]{1,0:T(8,128)S(1)} %divide_subtract_fusion.2), channel_id=1, source_target_pairs={{0,4},{4,8},{8,12},{12,0},{1,5},{5,9},{9,13},{13,1},{2,6},{6,10},{... | collective-permute-start | bytes 196616 | tf_op jit(solution)/shard_map/ppermute | solution.py:15
Sparse Core Ops, SparseCore 0:
  23.1 22.0 reduce-scatter.2
  76.7 18.8 reduce-scatter.4
